TPU v7x, 32 devices: a whole 2x2x4 slice. The times are simulated.
32 devices in a mesh: groups: 2 (over y), sky: 16 (over z, x, core).
Axes of the slice: x: 2, y: 2, z: 4, core: 2. Of those that a mesh axis runs over, the one named last changes fastest.
Arguments:
- model: float32 [64, 6, 256, 128], P(('groups', 'sky')), parts along dimension 0, may hold values from 0 to 2
- exposures: bfloat16 [4096, 16, 128], P(('groups', 'sky')), parts along dimension 0, may hold values from -6 to 6
- inv_var: float32 [4096], P(('groups', 'sky')), parts along dimension 0, may hold values from 0.5 to 2
- step_size: float32 [6], replicated, may hold values from 0.2 to 0.6
- psf_taps: float32 [64, 56], P(('groups', 'sky')), parts along dimension 0, may hold values from 0.05 to 1
- exp_batch: int32 [4096], P(('groups', 'sky')), parts along dimension 0, may hold values from 0 to 31
- send_plane: int32 [512, 16], P(('groups', 'sky')), parts along dimension 0, may hold values from -1 to 11, as said below
- send_row: int32 [512, 16], P(('groups', 'sky')), parts along dimension 0, may hold values from 0 to 248, as said below
- send_cover: int32 [512, 16], P(('groups', 'sky')), parts along dimension 0, may hold values from 0 to 16, as said below
- use_slot: int32 [4096, 2], P(('groups', 'sky')), parts along dimension 0, may hold values from -1 to 255, as said below
- use_start: int32 [4096, 2], P(('groups', 'sky')), parts along dimension 0, may hold values from 0 to 8, as said below
- use_stop: int32 [4096, 2], P(('groups', 'sky')), parts along dimension 0, may hold values from 0 to 16
- foot_lo: int32 [64], P(('groups', 'sky')), parts along dimension 0, may hold values from 0 to 63
- foot_hi: int32 [64], P(('groups', 'sky')), parts along dimension 0, may hold values from 193 to 256
Outputs:
- updated_model: float32 [64, 6, 256, 128], P(('groups', 'sky')), parts along dimension 0
- residual: float32 [4096, 16, 128], P(('groups', 'sky')), parts along dimension 0
There are 2 independent parts, one for each index of `groups`. A program takes and returns all parts, laid end to end along the dimension named above; an argument that names none is the same for every part. Nothing has to cross between parts.
Inputs may be any that keep to these rules, and one draw needn't show every extreme that they name: In each row of send_plane the covered rows of the live slots (send_cover) sum to at most 128, and on every device some row reaches it. A live slot of exposure owner d is used by exactly one intersection of one exposure on d, and every intersection with use_slot >= 0 names a live slot; all pieces of an exposure come from planes of one band. `send_row`: for a live slot, the tile rows that its piece covers lie inside the tile. send_cover of a live slot equals use_stop - use_start of the intersection that uses it. `use_slot`: each exposure has 1 to 2 live intersections, first in order; -1 after them. `use_start`: the live intersections of an exposure cover rows 0 to 15 in order without gaps; dead ones have start and stop 0.
All inputs are finite; a program needn't handle non-finite values.
Results may differ from a plain program's by a relative error of at most 0.0011.
Values may be sent and summed in bfloat16 or wider, within the bound.
A program may use at most 128 MiB of HBM per device.

v0:
```python
import functools

import jax
import jax.numpy as jnp
import numpy as np
from jax import lax
from jax.experimental import pallas as pl
from jax.experimental.pallas import tpu as pltpu
from jax.sharding import PartitionSpec as P

NPSF = 4
TAPS = 7
ITERS = 2
F32 = jnp.float32
BF16 = jnp.bfloat16


def vmem():
    return pl.BlockSpec(memory_space=pltpu.VMEM)


def smem():
    return pl.BlockSpec(memory_space=pltpu.SMEM)


def pack_rows(image, packed, plane, row, cover, rows_each, tile_rows, height):
    peers, capacity = plane.shape

    def one_peer(o, carry):
        offset = o * rows_each
        for c in range(capacity):
            source = jnp.maximum(plane[o, c], 0) * tile_rows + row[o, c]
            packed[pl.ds(offset, height), :] = image[pl.ds(source, height), :]
            offset = offset + cover[o, c]
        return carry

    lax.fori_loop(0, peers, one_peer, 0)


def emit_packed(packed, out, rows_each):
    def one_peer(o, carry):
        start = pl.multiple_of(o * rows_each, 16)
        out[o, pl.ds(0, rows_each), :] = packed[pl.ds(start, rows_each), :].astype(BF16)
        return carry

    lax.fori_loop(0, out.shape[0], one_peer, 0)


def first_kernel(rows_each, tile_rows, height, plane, row, cover, model, banks, out, image, packed):
    total = model.shape[0]
    image[pl.ds(0, total), :] = model[...]
    image[pl.ds(total, height), :] = jnp.zeros((height, model.shape[1]), F32)
    pack_rows(image, packed, plane, row, cover, rows_each, tile_rows, height)
    emit_packed(packed, out, rows_each)
    extra = banks.shape[0]

    def add_banks(o, carry):
        out[o, pl.ds(rows_each, extra), :] = banks[...]
        return carry

    lax.fori_loop(0, out.shape[0], add_banks, 0)


def tile_kernel(rows_each, tile_rows, height, band_count, last, plane, row, cover, lo, hi, step, current,
                returned, *rest):
    if last:
        updated, grad, arrived = rest
    else:
        updated, out, grad, arrived, image, packed = rest
    total, columns = current.shape
    peers, capacity = plane.shape

    def clear(i, carry):
        start = pl.multiple_of(i * 64, 64)
        grad[pl.ds(start, 64), :] = jnp.zeros((64, columns), F32)
        return carry

    lax.fori_loop(0, total // 64, clear, 0)
    grad[pl.ds(total, height), :] = jnp.zeros((height, columns), F32)

    def widen(o, carry):
        start = pl.multiple_of(o * rows_each, 16)
        arrived[pl.ds(start, rows_each), :] = returned[o].astype(F32)
        return carry

    lax.fori_loop(0, peers, widen, 0)
    arrived[pl.ds(peers * rows_each, height), :] = jnp.zeros((height, columns), F32)
    position = lax.broadcasted_iota(jnp.int32, (height, columns), 0)

    def one_peer(o, carry):
        offset = o * rows_each
        for c in range(capacity):
            target = jnp.maximum(plane[o, c], 0) * tile_rows + row[o, c]
            count = cover[o, c]
            part = jnp.where(position < count, arrived[pl.ds(offset, height), :], 0.0)
            grad[pl.ds(target, height), :] += part
            offset = offset + count
        return carry

    lax.fori_loop(0, peers, one_peer, 0)
    tile_position = lax.broadcasted_iota(jnp.int32, (tile_rows, columns), 0)

    def one_plane(p, carry):
        tile = p // band_count
        start = pl.multiple_of(p * tile_rows, 8)
        here = pl.ds(start, tile_rows)
        moved = jnp.maximum(current[here, :] - step[p % band_count] * grad[here, :], 0.0)
        moved = jnp.where((tile_position >= lo[tile]) & (tile_position < hi[tile]), moved, 0.0)
        updated[here, :] = moved
        if not last:
            image[here, :] = moved
        return carry

    lax.fori_loop(0, total // tile_rows, one_plane, 0)
    if not last:
        image[pl.ds(total, height), :] = jnp.zeros((height, columns), F32)
        pack_rows(image, packed, plane, row, cover, rows_each, tile_rows, height)
        emit_packed(packed, out, rows_each)


def spread(value, target, direction, masks):
    height, columns = value.shape
    half = TAPS // 2
    for v in range(TAPS):
        shift = direction * (v - half)
        part = value
        if shift != 0:
            part = jnp.where(masks[shift + half], pltpu.roll(value, shift % columns, 1), 0.0)
        target[pl.ds(v * height, height), :] = part.astype(BF16)


def apply(operators, bank, way, shifted):
    operator = jnp.concatenate([operators[bank, 0, way], operators[bank, 1, way]], axis=0)
    both = jnp.dot(operator, shifted, preferred_element_type=F32)
    height = both.shape[0] // 2
    return both[:height] + both[height:]


def exposure_kernel(rows_each, unroll, last, at, first, batch, weight, begin, source, arrived, operators, observed,
                    *rest):
    if last:
        residual, out, gathered, stamps, forward, backward = rest
    else:
        out, gathered, stamps, forward, backward = rest
    count, height, columns = observed.shape
    peers = out.shape[0]
    meets = at.shape[0]
    capacity = begin.shape[0] // peers
    half = TAPS // 2

    gathered[pl.ds(0, height), :] = jnp.zeros((height, columns), F32)
    gathered[pl.ds(height + peers * rows_each, height), :] = jnp.zeros((height, columns), F32)
    stamps[pl.ds(count * height, height), :] = jnp.zeros((height, columns), F32)
    used = TAPS * height
    spare = forward.shape[1] - used
    if spare:
        for i in range(unroll):
            forward[i, pl.ds(used, spare), :] = jnp.zeros((spare, columns), BF16)
            backward[i, pl.ds(used, spare), :] = jnp.zeros((spare, columns), BF16)

    def widen(o, carry):
        here = pl.multiple_of(o * rows_each + height, 8)
        gathered[pl.ds(here, rows_each), :] = arrived[o, pl.ds(0, rows_each), :].astype(F32)
        return carry

    lax.fori_loop(0, peers, widen, 0)
    position = lax.broadcasted_iota(jnp.int32, (height, columns), 0)
    lane = lax.broadcasted_iota(jnp.int32, (height, columns), 1)
    masks = [
        (lane >= shift) if shift > 0 else (lane < columns + shift) for shift in range(-half, half + 1)
    ]

    def assemble(e):
        value = None
        for k in range(meets):
            piece = gathered[pl.ds(at[k, e], height), :]
            value = piece if value is None else jnp.where(position >= first[k, e], piece, value)
        return value

    def group(g, carry):
        which = [g * unroll + i for i in range(unroll)]
        for i, e in enumerate(which):
            spread(assemble(e), forward.at[i], 1, masks)
        for i, e in enumerate(which):
            predicted = apply(operators, batch[e], 0, forward[i])
            error = weight[e] * (predicted - observed[e].astype(F32))
            if last:
                residual[e] = error
            spread(error, backward.at[i], -1, masks)
        for i, e in enumerate(which):
            here = pl.multiple_of(e * height, 8)
            stamps[pl.ds(here, height), :] = apply(operators, batch[e], 1, backward[i])
        return carry

    lax.fori_loop(0, count // unroll, group, 0)

    def give(o, carry):
        for c in range(capacity):
            name = o * capacity + c
            gathered[pl.ds(begin[name], height), :] = stamps[pl.ds(source[name], height), :]
        return carry

    lax.fori_loop(0, peers, give, 0)
    emit_packed(gathered, out, rows_each)


def slot_tables(rows_each, height, peers, capacity, use_slot, use_start, use_stop):
    slots = peers * capacity
    names, start, stop = use_slot.T, use_start.T, use_stop.T
    alive = names >= 0
    first = jnp.where(alive, start, height)
    flat = names.reshape(-1)
    length = jnp.where(alive, stop - start, 0).reshape(-1)
    every = jnp.concatenate([jnp.arange(slots, dtype=jnp.int32), flat])
    peer = jnp.maximum(every, 0) // capacity
    earlier = (flat[None, :] >= (peer * capacity)[:, None]) & (flat[None, :] < every[:, None])
    begin = peer * rows_each + jnp.sum(jnp.where(earlier, length[None, :], 0), axis=1)
    row = (jnp.arange(names.shape[1], dtype=jnp.int32) * height)[None, :] + start
    same = flat[None, :] == jnp.arange(slots, dtype=jnp.int32)[:, None]
    source = jnp.sum(jnp.where(same, row.reshape(1, -1), 0), axis=1)
    at = height + jnp.where(alive, begin[slots:].reshape(names.shape) - first, 0)
    return at, first, begin[:slots], source


def partner(me, i, peers):
    if peers & (peers - 1):
        return lax.rem(me + i, peers)
    other = me
    bit = 1
    while bit < peers:
        if i & bit:
            other = other + (1 - 2 * lax.rem(me // bit, 2)) * bit
        bit *= 2
    return other


def exchange_kernel(outgoing, incoming, send_sems, recv_sems, own_sem):
    me = lax.axis_index("sky")
    peers = outgoing.shape[0]
    order = [base + d for base in range(0, peers, 4) for d in (2, 0, 3, 1) if 0 < base + d < peers]
    barrier = pltpu.get_barrier_semaphore()
    for i in order:
        pl.semaphore_signal(
            barrier, inc=1, device_id={"sky": partner(me, i, peers)}, device_id_type=pl.DeviceIdType.MESH
        )
    pl.semaphore_wait(barrier, peers - 1)
    copies = []
    for i in order:
        to = partner(me, i, peers)
        copy = pltpu.make_async_remote_copy(
            src_ref=outgoing.at[to],
            dst_ref=incoming.at[me],
            send_sem=send_sems.at[i],
            recv_sem=recv_sems.at[i],
            device_id={"sky": to},
            device_id_type=pl.DeviceIdType.MESH,
        )
        copy.start()
        copies.append(copy)
    own = pltpu.make_async_copy(outgoing.at[me], incoming.at[me], own_sem)
    own.start()
    own.wait()
    for copy in copies:
        copy.wait()


def exchange(outgoing, ident):
    peers = outgoing.shape[0]
    return pl.pallas_call(
        exchange_kernel,
        out_shape=jax.ShapeDtypeStruct(outgoing.shape, outgoing.dtype),
        in_specs=[pl.BlockSpec(memory_space=pl.ANY)],
        out_specs=pl.BlockSpec(memory_space=pl.ANY),
        scratch_shapes=[
            pltpu.SemaphoreType.DMA((peers,)),
            pltpu.SemaphoreType.DMA((peers,)),
            pltpu.SemaphoreType.DMA,
        ],
        compiler_params=pltpu.CompilerParams(collective_id=ident, has_side_effects=True),
        name="exchange",
    )(outgoing)


def operator_pattern(height, depth):
    half = TAPS // 2
    pattern = np.zeros((TAPS * TAPS, 2, height, depth), np.float32)
    for v in range(TAPS):
        for a in range(height):
            for s in range(height):
                if abs(a - s) <= half:
                    pattern[(a - s + half) * TAPS + v, 0, a, v * height + s] = 1.0
                    pattern[(s - a + half) * TAPS + v, 1, a, v * height + s] = 1.0
    return pattern.reshape(TAPS * TAPS, -1)


def point_spread(psf_taps):
    own_banks = psf_taps.shape[0]
    taps = psf_taps.reshape(own_banks, 2, NPSF, TAPS)
    taps = lax.reduce_precision(taps / jnp.sum(taps, axis=-1, keepdims=True), 8, 7)
    kernels = jnp.sum(taps[:, 0, :, :, None] * taps[:, 1, :, None, :], axis=1) / NPSF
    kernels = kernels.reshape(own_banks, TAPS * TAPS)
    coarse = lax.reduce_precision(kernels, 8, 7)
    return jnp.concatenate([coarse, kernels - coarse], axis=1).astype(BF16)


def build_operators(halves, height, depth):
    pattern = jnp.asarray(operator_pattern(height, depth), BF16)
    full = jnp.dot(halves.reshape(-1, TAPS * TAPS), pattern, preferred_element_type=F32).astype(BF16)
    return full.reshape(-1, 2, 2, height, depth)


def body(model, exposures, inv_var, step_size, psf_taps, exp_batch, send_plane, send_row, send_cover, use_slot,
         use_start, use_stop, foot_lo, foot_hi):
    tile_count, band_count, tile_rows, columns = model.shape
    count, height, _ = exposures.shape
    peers, capacity = send_plane.shape
    rows_each = capacity * height // 2
    total = tile_count * band_count * tile_rows
    packed_rows = peers * rows_each
    own_banks = psf_taps.shape[0]
    extra = -(-own_banks // 16) * 16
    depth = -(-TAPS * height // 128) * 128
    unroll = 32 if count % 32 == 0 else 1

    banks = point_spread(psf_taps)
    width = banks.shape[1]
    banks = jnp.pad(banks, ((0, extra - own_banks), (0, columns - width)))
    at, first, begin, source = slot_tables(rows_each, height, peers, capacity, use_slot, use_start, use_stop)

    image_scratch = pltpu.VMEM((total + height, columns), F32)
    packed_scratch = pltpu.VMEM((packed_rows + height, columns), F32)

    current = model.reshape(total, columns)
    outbound = pl.pallas_call(
        functools.partial(first_kernel, rows_each, tile_rows, height),
        out_shape=jax.ShapeDtypeStruct((peers, rows_each + extra, columns), BF16),
        in_specs=[smem()] * 3 + [vmem()] * 2,
        out_specs=vmem(),
        scratch_shapes=[image_scratch, packed_scratch],
        name="first_pack",
    )(send_plane, send_row, send_cover, current, banks)
    residual = None
    operators = None
    for sweep in range(ITERS):
        arrived = exchange(outbound, 0 if sweep == 0 else 1)
        if sweep == 0:
            halves = arrived[:, rows_each : rows_each + own_banks, :width]
            operators = build_operators(halves, height, depth)
        last = sweep == ITERS - 1
        residual_shape = jax.ShapeDtypeStruct(exposures.shape, F32)
        outgoing_shape = jax.ShapeDtypeStruct((peers, rows_each, columns), BF16)
        result = pl.pallas_call(
            functools.partial(exposure_kernel, rows_each, unroll, last),
            out_shape=(residual_shape, outgoing_shape) if last else outgoing_shape,
            in_specs=[smem()] * 6 + [vmem()] * 3,
            out_specs=(vmem(), vmem()) if last else vmem(),
            scratch_shapes=[
                pltpu.VMEM((packed_rows + 2 * height, columns), F32),
                pltpu.VMEM(((count + 1) * height, columns), F32),
                pltpu.VMEM((unroll, depth, columns), BF16),
                pltpu.VMEM((unroll, depth, columns), BF16),
            ],
            name="exposures_last" if last else "exposures",
        )(at, first, exp_batch, inv_var, begin, source, arrived, operators, exposures)
        if last:
            residual, outgoing = result
        else:
            outgoing = result
        returned = exchange(outgoing, 1)
        updated_shape = jax.ShapeDtypeStruct((total, columns), F32)
        outbound_shape = jax.ShapeDtypeStruct((peers, rows_each, columns), BF16)
        result = pl.pallas_call(
            functools.partial(tile_kernel, rows_each, tile_rows, height, band_count, last),
            out_shape=updated_shape if last else (updated_shape, outbound_shape),
            in_specs=[smem()] * 6 + [vmem()] * 2,
            out_specs=vmem() if last else (vmem(), vmem()),
            scratch_shapes=[image_scratch, packed_scratch] + ([] if last else [image_scratch, packed_scratch]),
            name="tiles_last" if last else "tiles",
        )(send_plane, send_row, send_cover, foot_lo, foot_hi, step_size, current, returned)
        if last:
            current = result
        else:
            current, outbound = result
    return current.reshape(model.shape), residual


def solution(mesh):
    both = ("groups", "sky")
    return jax.shard_map(
        body,
        mesh=mesh,
        in_specs=(
            P(both, None, None, None),
            P(both, None, None),
            P(both),
            P(),
            P(both, None),
            P(both),
            P(both, None),
            P(both, None),
            P(both, None),
            P(both, None),
            P(both, None),
            P(both, None),
            P(both),
            P(both),
        ),
        out_specs=(P(both, None, None, None), P(both, None, None)),
        check_vma=False,
    )
```

profile of v0, /device:TPU:0, one launch (start us, length us, event | category | flops | bytes accessed | tf_op | source)
XLA Modules:
  0.0 101.1 jit_solution(14799582904771825512)
XLA Ops:
  0.6 0.7 fusion.14
  1.4 0.7 broadcast_multiply_fusion.1
  2.1 1.0 select_reduce_fusion
  3.0 0.7 multiply_add_fusion
  3.7 0.6 slice.17.begin
  4.3 0.7 fusion.9
  5.0 1.3 %bitcast_select_fusion = (s32[2,128]{1,0:T(2,128)}, s32[2,128]{1,0:T(2,128)}, s32[256]{0:T(256)S(1)}) fusion(s32[128,2]{0,1:T(2,128)} %param.25, s32[128,2]{0,1:T(2,128)} %param.24, s32[4,128]{1,0:T(4,128)S(1)} %fusion.9, s32[128]{0:T(128)S(1)} %iota_multiply_fusion), kind=kLoop, calls=%fused_computation.36 | loop fusion | flops 1536 | bytes 6656 | tf_op jit(solution)/shard_map/jit(_where)/select_n | solution.py:211
  6.3 1.4 %select_reduce_fusion.1.source = s32[256]{0:T(256)} fusion(s32[256]{0:T(256)S(1)} %get-tuple-element.18, s32[256]{0:T(256)} %bitcast.52), kind=kLoop, calls=%fused_computation.3 | loop fusion | flops 196352 | bytes 3072 | tf_op jit(solution)/shard_map/reduce_sum | solution.py:220
  7.7 0.8 reshape.65
  8.4 0.1 divide_reduce-precision_fusion
  8.5 0.1 copy.17
  8.6 0.1 multiply_reduce_fusion
  8.8 0.1 div.36
  8.8 0.7 fusion.6.banks
  9.5 0.0 copy-start
  9.5 3.6 %first_pack.1.outgoing = bf16[16,144,128]{2,1,0:T(8,128)(2,1)} custom-call(s32[16,16]{1,0:T(8,128)} %plane.5, s32[16,16]{1,0:T(8,128)} %row.5, s32[16,16]{1,0:T(8,128)} %cover.5, f32[3072,128]{1,0:T(8,128)} %bitcast.43, bf16[16,128]{1,0:T(8,128)(2,1)} %fusion.6.banks), custom_call_target="tpu_custom_call" | custom-call | tf_op jit(solution)/shard_map/first_pack/pallas_call | solution.py:334
  13.1 17.1 %exchange.4.arrived = bf16[16,144,128]{2,1,0:T(8,128)(2,1)} custom-call(bf16[16,144,128]{2,1,0:T(8,128)(2,1)} %first_pack.1.outgoing), custom_call_target="tpu_custom_call" | custom-call | tf_op jit(solution)/shard_map/exchange/pallas_call | solution.py:269
  30.2 0.8 slice.20
  31.0 0.1 reshape.66
  31.1 0.0 copy-done
  31.1 0.3 fusion
  31.4 0.9 copy.18
  32.3 5.9 %exposures.1.outgoing = bf16[16,128,128]{2,1,0:T(8,128)(2,1)} custom-call(s32[2,128]{1,0:T(2,128)} %get-tuple-element.13.at, s32[2,128]{1,0:T(2,128)} %get-tuple-element.12.first, s32[128]{0:T(128)} %batch.3, f32[128]{0:T(128)} %weight.3, s32[256]{0:T(256)} %slice.17.begin, s32[256]{0:T(256)} %select_reduce_fusion.1.source, ...), custom_call_target="tpu_custom_call" | custom-call | tf_op jit(solution)/shard_map/exposures/pallas_call | solution.py:352
  38.2 16.1 %exchange.5.returned = bf16[16,128,128]{2,1,0:T(8,128)(2,1)} custom-call(bf16[16,128,128]{2,1,0:T(8,128)(2,1)} %exposures.1.outgoing), custom_call_target="tpu_custom_call" | custom-call | tf_op jit(solution)/shard_map/exchange/pallas_call | solution.py:269
  54.3 6.0 %tiles.1 = (f32[3072,128]{1,0:T(8,128)}, bf16[16,128,128]{2,1,0:T(8,128)(2,1)}) custom-call(s32[16,16]{1,0:T(8,128)} %plane.5, s32[16,16]{1,0:T(8,128)} %row.5, s32[16,16]{1,0:T(8,128)} %cover.5, s32[2]{0:T(128)} %lo.3, s32[2]{0:T(128)} %hi.3, f32[6]{0:T(128)} %step.3, f32[3072,128]{1,0:T(8,128)} %bitcast.44, bf16[16,128,128]{2,1,0:T(8,128)(2,1)} %exchange.5.returned), custom_call_target="tpu_custom_call" | custom-call | tf_op jit(solution)/shard_map/tiles/pallas_call | solution.py:372
  60.3 14.9 %exchange.6.arrived = bf16[16,128,128]{2,1,0:T(8,128)(2,1)} custom-call(bf16[16,128,128]{2,1,0:T(8,128)(2,1)} %get-tuple-element.7.outgoing), custom_call_target="tpu_custom_call" | custom-call | tf_op jit(solution)/shard_map/exchange/pallas_call | solution.py:269
  75.2 6.3 %exposures_last.1 = (f32[128,16,128]{2,1,0:T(8,128)}, bf16[16,128,128]{2,1,0:T(8,128)(2,1)}) custom-call(s32[2,128]{1,0:T(2,128)} %get-tuple-element.13.at, s32[2,128]{1,0:T(2,128)} %get-tuple-element.12.first, s32[128]{0:T(128)} %batch.3, f32[128]{0:T(128)} %weight.3, s32[256]{0:T(256)} %slice.17.begin, s32[256]{0:T(256)} %select_reduce_fusion.1.source, ...), custom_call_target="tpu_custom_call" | custom-call | tf_op jit(solution)/shard_map/exposures_last/pallas_call | solution.py:352
  81.5 14.9 %exchange.7.returned = bf16[16,128,128]{2,1,0:T(8,128)(2,1)} custom-call(bf16[16,128,128]{2,1,0:T(8,128)(2,1)} %get-tuple-element.8.outgoing), custom_call_target="tpu_custom_call" | custom-call | tf_op jit(solution)/shard_map/exchange/pallas_call | solution.py:269
  96.4 4.7 %tiles_last.1 = f32[3072,128]{1,0:T(8,128)} custom-call(s32[16,16]{1,0:T(8,128)} %plane.5, s32[16,16]{1,0:T(8,128)} %row.5, s32[16,16]{1,0:T(8,128)} %cover.5, s32[2]{0:T(128)} %lo.3, s32[2]{0:T(128)} %hi.3, f32[6]{0:T(128)} %step.3, f32[3072,128]{1,0:T(8,128)} %get-tuple-element.6.current, bf16[16,128,128]{2,1,0:T(8,128)(2,1)} %exchange.7.returned), custom_call_target="tpu_custom_call" | custom-call | tf_op jit(solution)/shard_map/tiles_last/pallas_call | solution.py:372
  (6 shorter events, 0.0 us)
Async XLA Ops:
  9.5 21.6 %copy-start = (bf16[49,4096]{1,0:T(8,128)(2,1)S(1)}, bf16[49,4096]{1,0:T(8,128)(2,1)}, u32[]{:S(2)}) copy-start(bf16[49,4096]{1,0:T(8,128)(2,1)} %constant.41.clone) | copy-start | bytes 1204228
where the time goes:
time: 102 us; the launch traced here: 101 us
  Pallas kernels  89.5 us (88%)
  other arithmetic  7.3 us (7%)
  local copies, waits for them, and re-layouts  3.29 us (3%)
    pallas_call x4, Pallas kernels, exchange(): pl.pallas_call(exchange_kernel, out_shape=jax.ShapeDtypeStruct(outgoing.s...  63 us
    pallas_call x2, Pallas kernels, body(): pl.pallas_call(functools.partial(exposure_kernel, rows_each, unroll, last...  12.2 us
    pallas_call x2, Pallas kernels, body(): pl.pallas_call(functools.partial(tile_kernel, rows_each, tile_rows, heigh...  10.8 us
    pallas_call x1, Pallas kernels, body(): pl.pallas_call(functools.partial(first_kernel, rows_each, tile_rows, heig...  3.56 us

commit v1 on v0

v1 whole, which is shorter than its diff:
```python
import functools

import jax
import jax.numpy as jnp
from jax import lax
from jax.experimental import pallas as pl
from jax.experimental.pallas import tpu as pltpu
from jax.sharding import PartitionSpec as P

NPSF = 4
TAPS = 7
ITERS = 2
F32 = jnp.float32
BF16 = jnp.bfloat16
I32 = jnp.int32


def vmem():
    return pl.BlockSpec(memory_space=pltpu.VMEM)


def hbm():
    return pl.BlockSpec(memory_space=pltpu.HBM)


def round_up(value, multiple):
    return -(-value // multiple) * multiple


def partner(me, i, peers):
    other = 0
    bit = 1
    while bit < peers:
        other = other + lax.rem(lax.div(me, bit) + lax.div(i, bit), 2) * bit
        bit *= 2
    return other


def iota(shape, axis):
    return lax.broadcasted_iota(I32, shape, axis)


def floor_div(value, divisor):
    return jnp.floor((value.astype(F32) + 0.5) * (1.0 / divisor))


def send_table(plane, row, cover, width, tile_rows):
    peers, capacity = plane.shape
    position = iota((peers, width), 1)
    chosen = jnp.zeros((peers, width), I32)
    offset = jnp.zeros((peers, 1), I32)
    for c in range(capacity):
        first = jnp.maximum(plane[:, c : c + 1], 0) * tile_rows + row[:, c : c + 1] - offset
        chosen = jnp.where(position >= offset, first + position, chosen)
        offset = offset + cover[:, c : c + 1]
    return chosen, position < offset


def use_tables(slot, start, stop, peers, capacity, rows_each, width, height):
    meets, count = slot.shape
    which_peer = iota((peers, count), 0).astype(F32)
    exposure = iota((1, count), 1).astype(F32)
    owners, columns, starts, lengths, alive, peer_rows = [], [], [], [], [], []
    for k in range(meets):
        name = slot[k : k + 1, :].astype(F32)
        peer = floor_div(name, capacity)
        owners.append(jnp.where(which_peer == peer, 1.0, 0.0))
        columns.append(name - peer * capacity)
        starts.append(start[k : k + 1, :].astype(F32))
        lengths.append(stop[k : k + 1, :].astype(F32) - starts[k])
        alive.append(name >= 0.0)
        peer_rows.append(peer)
    begin = jnp.zeros((peers, 1), F32)
    found = [jnp.zeros((1, count), F32) for _ in range(meets)]
    position = iota((peers, width), 1).astype(F32)
    chosen = jnp.zeros((peers, width), F32)
    for c in range(capacity):
        length = jnp.zeros((peers, count), F32)
        source = jnp.zeros((peers, count), F32)
        for k in range(meets):
            here = jnp.where(columns[k] == c, owners[k], 0.0)
            length = length + here * lengths[k]
            source = source + here * (exposure * height + starts[k])
            found[k] = found[k] + jnp.sum(here * begin, axis=0, keepdims=True)
        source = jnp.sum(source, axis=1, keepdims=True)
        chosen = jnp.where(position >= begin, source - begin + position, chosen)
        begin = begin + jnp.sum(length, axis=1, keepdims=True)
    give = jnp.clip(chosen.astype(I32), 0, count * height - 1)
    rows = []
    for k in range(meets):
        where = height + peer_rows[k] * rows_each + found[k] - starts[k]
        rows.append(jnp.where(alive[k], where, float(height)))
    for k in range(meets):
        rows.append(jnp.where(alive[k], starts[k], float(height)))
    limits = [peers * rows_each + height] * meets + [height] * meets
    return give, [jnp.clip(value.astype(I32), 0, limit) for value, limit in zip(rows, limits)]


def spread(value, target, direction, masks):
    height, columns = value.shape
    half = TAPS // 2
    for v in range(TAPS):
        shift = direction * (v - half)
        part = value
        if shift != 0:
            part = jnp.where(masks[shift + half], pltpu.roll(value, shift % columns, 1), 0.0)
        target[pl.ds(v * height, height), :] = part.astype(BF16)


def apply(operator, shifted):
    both = jnp.dot(operator, shifted, preferred_element_type=F32)
    height = both.shape[0] // 2
    return both[:height] + both[height:]


def build_operators(taps, expanded, operators, height):
    banks, lanes = taps.shape
    used = 2 * NPSF * TAPS
    group_row = floor_div(iota((lanes, lanes), 0), TAPS)
    group_column = floor_div(iota((lanes, lanes), 1), TAPS)
    lane = iota((lanes, lanes), 1)
    together = jnp.where((group_row == group_column) & (lane < used), 1.0, 0.0)
    raw = taps[...]
    sums = jnp.dot(raw, together, precision=lax.Precision.HIGHEST, preferred_element_type=F32)
    scaled = jnp.where(iota((banks, lanes), 1) < used, raw / jnp.where(sums > 0.0, sums, 1.0), 0.0)
    scaled = scaled.astype(BF16)
    depth = operators.shape[-1]
    tap_of = floor_div(iota((lanes, depth), 1), height).astype(I32)
    column_taps = []
    for j in range(NPSF):
        pick = (iota((lanes, depth), 0) == (NPSF + j) * TAPS + tap_of) & (tap_of < TAPS)
        pick = jnp.where(pick, 1.0, 0.0).astype(BF16)
        column_taps.append(jnp.dot(scaled, pick, preferred_element_type=F32))
    scaled = scaled.astype(F32)
    for u in range(TAPS):
        kernel = jnp.zeros((banks, depth), F32)
        for j in range(NPSF):
            at = j * TAPS + u
            kernel = kernel + scaled[:, at : at + 1] * column_taps[j]
        kernel = kernel * (1.0 / NPSF)
        coarse = kernel.astype(BF16).astype(F32)
        expanded[u, :, :] = coarse
        expanded[TAPS + u, :, :] = kernel - coarse
    lane = iota((height, depth), 1)
    tap = floor_div(lane, height).astype(I32)
    difference = iota((height, depth), 0) - (lane - tap * height)
    inside = tap < TAPS
    half = TAPS // 2

    def one_bank(b, carry):
        for part in range(2):
            ways = [jnp.zeros((height, depth), F32) for _ in range(2)]
            for u in range(TAPS):
                value = expanded[part * TAPS + u, pl.ds(b, 1), :]
                ways[0] = jnp.where(inside & (difference == u - half), value, ways[0])
                ways[1] = jnp.where(inside & (difference == half - u), value, ways[1])
            for way in range(2):
                operators[b, way, pl.ds(part * height, height), :] = ways[way].astype(BF16)
        return carry

    lax.fori_loop(0, banks, one_bank, 0)


def kernel(tile_rows, band_count, unroll, batch_in, weight_in, lo_in, hi_in, step_in, plane_in, row_in, cover_in,
           slot_in, start_in, stop_in, psf_in, exposures, model, updated, residual, batch, weight, lo, hi, step, plane,
           row, cover, slot, start, stop, psf, observed, image, grad, gathered, stamps, forward, backward, rows_out,
           leaving, landing, taps_out, taps_in, taps, expanded, operators, tables, targets, plane_ids, plane_of,
           indices, send_sems, recv_sems, own_sems):
    me = lax.axis_index("sky")
    peers, capacity = plane.shape
    total, columns = image.shape
    count, height, _ = observed.shape
    rows_each = landing.shape[2]
    meets = slot.shape[0]
    width = tables.shape[1]
    own_banks = psf.shape[0]
    half = TAPS // 2
    last = peers - 1

    barrier = pltpu.get_barrier_semaphore()

    def greet(i, carry):
        pl.semaphore_signal(
            barrier, inc=1, device_id={"sky": partner(me, i, peers)}, device_id_type=pl.DeviceIdType.MESH
        )
        return carry

    lax.fori_loop(1, peers, greet, 0)
    pairs = [(plane_in, plane), (row_in, row), (cover_in, cover), (slot_in, slot), (start_in, start), (stop_in, stop),
             (psf_in, psf), (model, image), (batch_in, batch), (weight_in, weight), (lo_in, lo), (hi_in, hi),
             (step_in, step), (exposures, observed)]
    copies = [pltpu.make_async_copy(a, b, own_sems.at[n]) for n, (a, b) in enumerate(pairs)]
    for copy in copies:
        copy.start()
    for copy in copies[:7]:
        copy.wait()

    chosen, used_rows = send_table(plane[...], row[...], cover[...], width, tile_rows)
    tables[pl.ds(0, peers), :] = jnp.clip(chosen, 0, total - 1)
    of_plane = floor_div(chosen, tile_rows)
    plane_ids[...] = of_plane
    targets[...] = jnp.where(used_rows, chosen - of_plane.astype(I32) * tile_rows, -1)
    give, at_rows = use_tables(slot[...], start[...], stop[...], peers, capacity, rows_each, width, height)
    tables[pl.ds(peers, peers), :] = give
    for k, value in enumerate(at_rows):
        tables[pl.ds(2 * peers + k, 1), pl.ds(0, count)] = value
    index_copy = pltpu.make_async_copy(tables, indices, own_sems.at[len(pairs)])
    index_copy.start()

    taps_out[...] = jnp.zeros(taps_out.shape, F32)
    taps_out[pl.ds(0, own_banks), pl.ds(0, psf.shape[1])] = psf[...]
    gathered[pl.ds(0, height), :] = jnp.zeros((height, columns), F32)
    gathered[pl.ds(height + peers * rows_each, height), :] = jnp.zeros((height, columns), F32)
    used = TAPS * height
    spare = forward.shape[1] - used
    if spare:
        for i in range(unroll):
            forward[i, pl.ds(used, spare), :] = jnp.zeros((spare, columns), BF16)
            backward[i, pl.ds(used, spare), :] = jnp.zeros((spare, columns), BF16)
    position = iota((height, columns), 0)
    lane = iota((height, columns), 1)
    masks = [
        (lane >= shift) if shift > 0 else (lane < columns + shift) for shift in range(-half, half + 1)
    ]
    index_copy.wait()
    copies[7].wait()

    def remote(phase, i):
        to = partner(me, i, peers)
        return pltpu.make_async_remote_copy(
            src_ref=leaving.at[phase, to],
            dst_ref=landing.at[phase, me],
            send_sem=send_sems.at[phase, i],
            recv_sem=recv_sems.at[phase, i],
            device_id={"sky": to},
            device_id_type=pl.DeviceIdType.MESH,
        )

    def remote_taps(i):
        return pltpu.make_async_remote_copy(
            src_ref=taps_out,
            dst_ref=taps_in.at[me],
            send_sem=send_sems.at[2 * ITERS, i],
            recv_sem=recv_sems.at[2 * ITERS, i],
            device_id={"sky": partner(me, i, peers)},
            device_id_type=pl.DeviceIdType.MESH,
        )

    def pick_rows(source, table_first, to):
        for p in range(rows_each):
            rows_out[pl.ds(p, 1), :] = source[pl.ds(indices[table_first + to, p], 1), :]
        return rows_out[...].astype(BF16)

    def send_all(phase, source, table_first):
        def one(t, carry):
            i = last - t
            to = partner(me, i, peers)
            leaving[phase, to, :, :] = pick_rows(source, table_first, to)

            @pl.when(t > 0)
            def _():
                remote(phase, i + 1).start()

            return carry

        lax.fori_loop(0, last, one, 0)
        landing[phase, me, :, :] = pick_rows(source, table_first, me)
        remote(phase, 1).start()

    def wait_barrier():
        pl.semaphore_wait(barrier, last)

        def one(t, carry):
            remote_taps(last - t).start()
            return carry

        lax.fori_loop(0, last, one, 0)
        taps_in[me, :, :] = taps_out[...]

    def take_taps():
        def one(t, carry):
            remote_taps(last - t).wait_recv()
            return carry

        lax.fori_loop(0, last, one, 0)

        def place(o, carry):
            taps[pl.ds(o * own_banks, own_banks), :] = taps_in[o, pl.ds(0, own_banks), :]
            return carry

        lax.fori_loop(0, peers, place, 0)
        build_operators(taps, expanded, operators, height)
        for copy in copies[8:]:
            copy.wait()

    def take_pieces(phase):
        def one(t, carry):
            i = last - t
            origin = partner(me, i, peers)

            @pl.when(i > 0)
            def _():
                remote(phase, i).wait_recv()

            here = pl.multiple_of(height + origin * rows_each, 8)
            gathered[pl.ds(here, rows_each), :] = landing[phase, origin].astype(F32)
            return carry

        lax.fori_loop(0, peers, one, 0)

    def assemble(e):
        value = None
        for k in range(meets):
            piece = gathered[pl.ds(indices[2 * peers + k, e], height), :]
            first = indices[2 * peers + meets + k, e]
            value = piece if value is None else jnp.where(position >= first, piece, value)
        return value

    def deblend():
        def group(g, carry):
            which = [g * unroll + i for i in range(unroll)]
            for i, e in enumerate(which):
                spread(assemble(e), forward.at[i], 1, masks)
            for i, e in enumerate(which):
                predicted = apply(operators[batch[e], 0], forward[i])
                error = weight[e] * (predicted - observed[e].astype(F32))
                residual[e] = error
                spread(error, backward.at[i], -1, masks)
            for i, e in enumerate(which):
                here = pl.multiple_of(e * height, 8)
                stamps[pl.ds(here, height), :] = apply(operators[batch[e], 1], backward[i])
            return carry

        lax.fori_loop(0, count // unroll, group, 0)

    together = 4 if rows_each % 128 == 0 and peers % 4 == 0 else 1
    planes = total // tile_rows
    wide = 2 if planes % 2 == 0 else 1

    def spread_planes():
        eye = iota((rows_each, width), 0) == iota((rows_each, width), 1)

        def one(o, carry):
            ids = jnp.where(eye, plane_ids[pl.ds(o, 1), :], 0.0)
            ids = jnp.sum(ids, axis=1, keepdims=True)
            plane_of[o, :, :] = jnp.broadcast_to(ids, (rows_each, columns)).astype(BF16)
            return carry

        lax.fori_loop(0, peers, one, 0)

    def clear():
        def one(p, carry):
            grad[p, :, :] = jnp.zeros((tile_rows, columns), F32)
            return carry

        lax.fori_loop(0, planes, one, 0)

    def joined(values, axis):
        return values[0] if len(values) == 1 else jnp.concatenate(values, axis=axis)

    def add_returned(phase):
        def one(q, carry):
            names, parts, owners = [], [], []
            for j in range(together):
                i = last - (q * together + j)
                origin = partner(me, i, peers)

                @pl.when(i > 0)
                def _():
                    remote(phase, i).wait_recv()

                names.append(targets[pl.ds(origin, 1), :][:, :rows_each])
                parts.append(landing[phase, origin])
                owners.append(plane_of[origin])
            name, part, owner = joined(names, 1), joined(parts, 0), joined(owners, 0)
            hit = iota((tile_rows, name.shape[1]), 0) == name
            chosen = jnp.where(hit, 1.0, 0.0).astype(BF16)
            for p in range(0, planes, wide):
                mine = [jnp.where(owner == float(p + w), part, jnp.zeros_like(part)) for w in range(wide)]
                both = jnp.dot(chosen, joined(mine, 1), preferred_element_type=F32)
                for w in range(wide):
                    grad[p + w, :, :] += both[:, w * columns : (w + 1) * columns]
            return carry

        lax.fori_loop(0, peers // together, one, 0)

    tile_position = iota((tile_rows, columns), 0)

    def move(target):
        def one_plane(p, carry):
            tile = lax.div(p, band_count)
            here = pl.ds(pl.multiple_of(p * tile_rows, 8), tile_rows)
            moved = jnp.maximum(image[here, :] - step[lax.rem(p, band_count)] * grad[p], 0.0)
            moved = jnp.where((tile_position >= lo[tile]) & (tile_position < hi[tile]), moved, 0.0)
            target[here, :] = moved
            return carry

        lax.fori_loop(0, total // tile_rows, one_plane, 0)

    wait_barrier()
    for sweep in range(ITERS):
        send_all(2 * sweep, image, 0)
        if sweep == 0:
            spread_planes()
            take_taps()
        take_pieces(2 * sweep)
        deblend()
        send_all(2 * sweep + 1, stamps, peers)
        clear()
        add_returned(2 * sweep + 1)
        move(updated if sweep == ITERS - 1 else image)

    def drain(t, carry):
        for phase in range(2 * ITERS):
            remote(phase, last - t).wait_send()
        remote_taps(last - t).wait_send()
        return carry

    lax.fori_loop(0, last, drain, 0)


def body(model, exposures, inv_var, step_size, psf_taps, exp_batch, send_plane, send_row, send_cover, use_slot,
         use_start, use_stop, foot_lo, foot_hi):
    tile_count, band_count, tile_rows, columns = model.shape
    count, height, _ = exposures.shape
    peers, capacity = send_plane.shape
    meets = use_slot.shape[1]
    rows_each = capacity * height // 2
    total = tile_count * band_count * tile_rows
    packed_rows = peers * rows_each
    own_banks = psf_taps.shape[0]
    tap_rows = round_up(own_banks, 8)
    depth = round_up(TAPS * height, 128)
    unroll = 32 if count % 32 == 0 else 1
    width = round_up(max(rows_each, count), 128)
    table_rows = 2 * peers + round_up(2 * meets, 8)
    banks = peers * own_banks
    operands = (exp_batch, inv_var, foot_lo, foot_hi, step_size, send_plane, send_row, send_cover, use_slot.T,
                use_start.T, use_stop.T, psf_taps, exposures, model.reshape(total, columns))
    updated, residual = pl.pallas_call(
        functools.partial(kernel, tile_rows, band_count, unroll),
        out_shape=(
            jax.ShapeDtypeStruct((total, columns), F32),
            jax.ShapeDtypeStruct(exposures.shape, F32),
        ),
        in_specs=[hbm()] * len(operands),
        out_specs=(vmem(), vmem()),
        scratch_shapes=[pltpu.SMEM(value.shape, value.dtype) for value in operands[:5]]
        + [pltpu.VMEM(value.shape, value.dtype) for value in operands[5:]]
        + [
            pltpu.VMEM((tile_count * band_count, tile_rows, columns), F32),
            pltpu.VMEM((packed_rows + 2 * height, columns), F32),
            pltpu.VMEM((count * height, columns), F32),
            pltpu.VMEM((unroll, depth, columns), BF16),
            pltpu.VMEM((unroll, depth, columns), BF16),
            pltpu.VMEM((rows_each, columns), F32),
            pltpu.VMEM((2 * ITERS, peers, rows_each, columns), BF16),
            pltpu.VMEM((2 * ITERS, peers, rows_each, columns), BF16),
            pltpu.VMEM((tap_rows, 128), F32),
            pltpu.VMEM((peers, tap_rows, 128), F32),
            pltpu.VMEM((banks, 128), F32),
            pltpu.VMEM((2 * TAPS, banks, depth), F32),
            pltpu.VMEM((banks, 2, 2 * height, depth), BF16),
            pltpu.VMEM((table_rows, width), I32),
            pltpu.VMEM((peers, width), I32),
            pltpu.VMEM((peers, width), F32),
            pltpu.VMEM((peers, rows_each, columns), BF16),
            pltpu.SMEM((table_rows, width), I32),
            pltpu.SemaphoreType.DMA((2 * ITERS + 1, peers)),
            pltpu.SemaphoreType.DMA((2 * ITERS + 1, peers)),
            pltpu.SemaphoreType.DMA((len(operands) + 1,)),
        ],
        compiler_params=pltpu.CompilerParams(
            collective_id=0, has_side_effects=True, vmem_limit_bytes=24 * 1024 * 1024
        ),
        name="deblend",
    )(*[pltpu.with_memory_space_constraint(value, pltpu.HBM) for value in operands])
    return updated.reshape(model.shape), residual


def solution(mesh):
    both = ("groups", "sky")
    return jax.shard_map(
        body,
        mesh=mesh,
        in_specs=(
            P(both, None, None, None),
            P(both, None, None),
            P(both),
            P(),
            P(both, None),
            P(both),
            P(both, None),
            P(both, None),
            P(both, None),
            P(both, None),
            P(both, None),
            P(both, None),
            P(both),
            P(both),
        ),
        out_specs=(P(both, None, None, None), P(both, None, None)),
        check_vma=False,
    )
```

time: 102 us -> 71.5 us (0.70)
  Pallas kernels: 89.5 us -> 68.6 us
  other arithmetic: 7.3 us -> 0 us
  local copies, waits for them, and re-layouts: 3.29 us -> 2.11 us
    pallas_call x9 -> x1, Pallas kernels: 89.5 us -> 68.6 us  [body(): pl.pallas_call(functools.partial(kernel, tile_rows, band_count, unroll),...]
    reduce_sum x3 -> x0, other arithmetic: 2.44 us -> none  [the longest x1 1.37 us: slot_tables(): source = jnp.sum(jnp.where(same, row.reshape(1, -1), 0), axis=1)]
    add x2 -> x0, other arithmetic: 1.39 us -> none  [slot_tables(): peer * rows_each + jnp.sum(jnp.where(earlier, length[None, :], 0), axis=1)]
    slice x2 -> x0, local copies, waits for them, and re-layouts: 1.36 us -> none  [the longest x1 0.77 us: body(): halves = arrived[:, rows_each:rows_each + own_banks, :width]]
    select_n x1 -> x0, other arithmetic: 1.28 us -> none  [slot_tables(): first = jnp.where(alive, start, height)]
    unnamed x3 -> x2, local copies, waits for them, and re-layouts: 0.9 us -> 2.11 us
where the time goes in v1:
time: 71.5 us; the launch traced here: 71.3 us
  Pallas kernels  68.6 us (96%)
  local copies, waits for them, and re-layouts  2.11 us (3%)
    pallas_call x1, Pallas kernels, body(): pl.pallas_call(functools.partial(kernel, tile_rows, band_count, unroll),...  68.6 us
    unnamed x2, local copies, waits for them, and re-layouts  2.11 us

profile of v1, /device:TPU:0, one launch (start us, length us, event | category | flops | bytes accessed | tf_op | source)
XLA Modules:
  0.0 71.3 jit_solution(2765640208885531658)
XLA Ops:
  0.6 68.6 %deblend.1 = (f32[3072,128]{1,0:T(8,128)S(1)}, f32[128,16,128]{2,1,0:T(8,128)S(1)}) custom-call(s32[128]{0:T(128)} %batch_in.1, f32[128]{0:T(128)} %weight_in.1, s32[2]{0:T(128)} %lo_in.1, s32[2]{0:T(128)} %hi_in.1, f32[6]{0:T(128)} %step_in.1, s32[16,16]{1,0:T(8,128)} %plane_in.1, s32[16,16]{1,0:T(8,128)} %row_in.1, s32[16,16]{1,0:T(8,128)} %cover_in.1, ...), custom_call_target="tpu_custom_call" | custom-call | tf_op jit(solution)/shard_map/deblend/pallas_call | solution.py:440
  69.2 1.1 %copy.18 = f32[2,6,256,128]{3,2,1,0:T(8,128)} copy(f32[2,6,256,128]{3,2,1,0:T(8,128)S(1)} %bitcast.5) | data formatting | bytes 3145728
  70.3 1.0 %copy.19 = f32[128,16,128]{2,1,0:T(8,128)} copy(f32[128,16,128]{2,1,0:T(8,128)S(1)} %get-tuple-element.9) | data formatting | bytes 2097152

commit v2 on v1

--- a/solution.py
+++ b/solution.py
@@ -293,9 +293,15 @@
         for copy in copies[8:]:
             copy.wait()
 
+    quarter = peers // 4 if peers % 4 == 0 else peers
+
+    def arrival(t):
+        block = lax.div(t, quarter)
+        return (lax.rem(3 * block, 5) - 2 * lax.div(block, 3)) * quarter + lax.rem(t, quarter)
+
     def take_pieces(phase):
         def one(t, carry):
-            i = last - t
+            i = arrival(t)
             origin = partner(me, i, peers)
 
             @pl.when(i > 0)
@@ -362,7 +368,7 @@
         def one(q, carry):
             names, parts, owners = [], [], []
             for j in range(together):
-                i = last - (q * together + j)
+                i = arrival(q * together + j)
                 origin = partner(me, i, peers)
 
                 @pl.when(i > 0)
@@ -417,6 +423,18 @@
         return carry
 
     lax.fori_loop(0, last, drain, 0)
+
+
+def emit_kernel(updated, residual, updated_out, residual_out, sems):
+    copies = []
+    for source, target in ((updated, updated_out), (residual, residual_out)):
+        rows = source.shape[0] // 4
+        for n in range(4):
+            part = pl.ds(n * rows, rows)
+            copies.append(pltpu.make_async_copy(source.at[part], target.at[part], sems.at[len(copies)]))
+            copies[-1].start()
+    for copy in copies:
+        copy.wait()
 
 
 def body(model, exposures, inv_var, step_size, psf_taps, exp_batch, send_plane, send_row, send_cover, use_slot,
@@ -475,6 +493,18 @@
         ),
         name="deblend",
     )(*[pltpu.with_memory_space_constraint(value, pltpu.HBM) for value in operands])
+    updated, residual = pl.pallas_call(
+        emit_kernel,
+        out_shape=(
+            jax.ShapeDtypeStruct((total, columns), F32),
+            jax.ShapeDtypeStruct(exposures.shape, F32),
+        ),
+        in_specs=[vmem()] * 2,
+        out_specs=(hbm(), hbm()),
+        scratch_shapes=[pltpu.SemaphoreType.DMA((8,))],
+        compiler_params=pltpu.CompilerParams(vmem_limit_bytes=1024 * 1024),
+        name="emit",
+    )(updated, residual)
     return updated.reshape(model.shape), residual
 
 

time: 71.5 us -> 68.6 us (0.959)
  local copies, waits for them, and re-layouts: 2.11 us -> 0 us
  Pallas kernels: 68.6 us -> 67.8 us
    pallas_call x1, Pallas kernels: 68.6 us -> 66.2 us  [body(): pl.pallas_call(functools.partial(kernel, tile_rows, band_count, unroll),...]
    unnamed x2 -> x0, local copies, waits for them, and re-layouts: 2.11 us -> none
    pallas_call x0 -> x1, Pallas kernels: none -> 1.55 us  [body(): pl.pallas_call(emit_kernel, out_shape=(jax.ShapeDtypeStruct((total, colum...]
where the time goes in v2:
time: 68.6 us; the launch traced here: 68.4 us
  Pallas kernels  67.8 us (99%)
    pallas_call x1, Pallas kernels, body(): pl.pallas_call(functools.partial(kernel, tile_rows, band_count, unroll),...  66.2 us
    pallas_call x1, Pallas kernels, body(): pl.pallas_call(emit_kernel, out_shape=(jax.ShapeDtypeStruct((total, colum...  1.55 us

profile of v2, /device:TPU:0, one launch (start us, length us, event | category | flops | bytes accessed | tf_op | source)
XLA Modules:
  0.0 68.4 jit_solution(11502448410167840021)
XLA Ops:
  0.6 66.2 %deblend.1 = (f32[3072,128]{1,0:T(8,128)S(1)}, f32[128,16,128]{2,1,0:T(8,128)S(1)}) custom-call(s32[128]{0:T(128)} %batch_in.1, f32[128]{0:T(128)} %weight_in.1, s32[2]{0:T(128)} %lo_in.1, s32[2]{0:T(128)} %hi_in.1, f32[6]{0:T(128)} %step_in.1, s32[16,16]{1,0:T(8,128)} %plane_in.1, s32[16,16]{1,0:T(8,128)} %row_in.1, s32[16,16]{1,0:T(8,128)} %cover_in.1, ...), custom_call_target="tpu_custom_call" | custom-call | tf_op jit(solution)/shard_map/deblend/pallas_call | solution.py:458
  66.9 1.6 %emit.1 = (f32[3072,128]{1,0:T(8,128)}, f32[128,16,128]{2,1,0:T(8,128)}) custom-call(f32[3072,128]{1,0:T(8,128)S(1)} %get-tuple-element.6.updated, f32[128,16,128]{2,1,0:T(8,128)S(1)} %get-tuple-element.7.residual), custom_call_target="tpu_custom_call" | custom-call | tf_op jit(solution)/shard_map/emit/pallas_call | solution.py:496

commit v3 on v2

--- a/solution.py
+++ b/solution.py
@@ -449,7 +449,7 @@
     own_banks = psf_taps.shape[0]
     tap_rows = round_up(own_banks, 8)
     depth = round_up(TAPS * height, 128)
-    unroll = 32 if count % 32 == 0 else 1
+    unroll = 64 if count % 64 == 0 else 1
     width = round_up(max(rows_each, count), 128)
     table_rows = 2 * peers + round_up(2 * meets, 8)
     banks = peers * own_banks

time: 68.6 us -> 67.8 us (0.988)
  Pallas kernels: 67.8 us -> 66.9 us
    pallas_call x1, Pallas kernels: 66.2 us -> 65.4 us  [body(): pl.pallas_call(functools.partial(kernel, tile_rows, band_count, unroll),...]
where the time goes in v3:
time: 67.8 us; the launch traced here: 67.6 us
  Pallas kernels  66.9 us (99%)
    pallas_call x1, Pallas kernels, body(): pl.pallas_call(functools.partial(kernel, tile_rows, band_count, unroll),...  65.4 us
    pallas_call x1, Pallas kernels, body(): pl.pallas_call(emit_kernel, out_shape=(jax.ShapeDtypeStruct((total, colum...  1.55 us

profile of v3, /device:TPU:0, one launch (start us, length us, event | category | flops | bytes accessed | tf_op | source)
XLA Modules:
  0.0 67.6 jit_solution(117970681413302850)
XLA Ops:
  0.6 65.4 %deblend.1 = (f32[3072,128]{1,0:T(8,128)S(1)}, f32[128,16,128]{2,1,0:T(8,128)S(1)}) custom-call(s32[128]{0:T(128)} %batch_in.1, f32[128]{0:T(128)} %weight_in.1, s32[2]{0:T(128)} %lo_in.1, s32[2]{0:T(128)} %hi_in.1, f32[6]{0:T(128)} %step_in.1, s32[16,16]{1,0:T(8,128)} %plane_in.1, s32[16,16]{1,0:T(8,128)} %row_in.1, s32[16,16]{1,0:T(8,128)} %cover_in.1, ...), custom_call_target="tpu_custom_call" | custom-call | tf_op jit(solution)/shard_map/deblend/pallas_call | solution.py:458
  66.0 1.6 %emit.1 = (f32[3072,128]{1,0:T(8,128)}, f32[128,16,128]{2,1,0:T(8,128)}) custom-call(f32[3072,128]{1,0:T(8,128)S(1)} %get-tuple-element.6.updated, f32[128,16,128]{2,1,0:T(8,128)S(1)} %get-tuple-element.7.residual), custom_call_target="tpu_custom_call" | custom-call | tf_op jit(solution)/shard_map/emit/pallas_call | solution.py:496

commit v4 on v3

--- a/solution.py
+++ b/solution.py
@@ -449,7 +449,7 @@
     own_banks = psf_taps.shape[0]
     tap_rows = round_up(own_banks, 8)
     depth = round_up(TAPS * height, 128)
-    unroll = 64 if count % 64 == 0 else 1
+    unroll = count
     width = round_up(max(rows_each, count), 128)
     table_rows = 2 * peers + round_up(2 * meets, 8)
     banks = peers * own_banks
@@ -489,7 +489,7 @@
             pltpu.SemaphoreType.DMA((len(operands) + 1,)),
         ],
         compiler_params=pltpu.CompilerParams(
-            collective_id=0, has_side_effects=True, vmem_limit_bytes=24 * 1024 * 1024
+            collective_id=0, has_side_effects=True, vmem_limit_bytes=40 * 1024 * 1024
         ),
         name="deblend",
     )(*[pltpu.with_memory_space_constraint(value, pltpu.HBM) for value in operands])

time: 67.8 us -> 67.4 us (level)
  no operation moved by 1% of the time
where the time goes in v4:
time: 67.4 us; the launch traced here: 67.1 us
  Pallas kernels  66.5 us (99%)
    pallas_call x1, Pallas kernels, body(): pl.pallas_call(functools.partial(kernel, tile_rows, band_count, unroll),...  65 us
    pallas_call x1, Pallas kernels, body(): pl.pallas_call(emit_kernel, out_shape=(jax.ShapeDtypeStruct((total, colum...  1.55 us

profile of v4, /device:TPU:0, one launch (start us, length us, event | category | flops | bytes accessed | tf_op | source)
XLA Modules:
  0.0 67.1 jit_solution(4424480119777042339)
XLA Ops:
  0.6 65.0 %deblend.1 = (f32[3072,128]{1,0:T(8,128)S(1)}, f32[128,16,128]{2,1,0:T(8,128)S(1)}) custom-call(s32[128]{0:T(128)} %batch_in.1, f32[128]{0:T(128)} %weight_in.1, s32[2]{0:T(128)} %lo_in.1, s32[2]{0:T(128)} %hi_in.1, f32[6]{0:T(128)} %step_in.1, s32[16,16]{1,0:T(8,128)} %plane_in.1, s32[16,16]{1,0:T(8,128)} %row_in.1, s32[16,16]{1,0:T(8,128)} %cover_in.1, ...), custom_call_target="tpu_custom_call" | custom-call | tf_op jit(solution)/shard_map/deblend/pallas_call | solution.py:458
  65.6 1.6 %emit.1 = (f32[3072,128]{1,0:T(8,128)}, f32[128,16,128]{2,1,0:T(8,128)}) custom-call(f32[3072,128]{1,0:T(8,128)S(1)} %get-tuple-element.6.updated, f32[128,16,128]{2,1,0:T(8,128)S(1)} %get-tuple-element.7.residual), custom_call_target="tpu_custom_call" | custom-call | tf_op jit(solution)/shard_map/emit/pallas_call | solution.py:496
